TPU v7x, 256 devices: a whole 4x4x8 slice. The times are simulated.
256 devices in a mesh: row: 16 (over z, core), col: 16 (over y, x).
Axes of the slice: x: 4, y: 4, z: 8, core: 2. Of those that a mesh axis runs over, the one named last changes fastest.
Arguments:
- clean_in: bfloat16 [512, 8192], P('row', 'col'), may hold values from -6 to 6
- corrupt_in: bfloat16 [512, 8192], P('row', 'col'), may hold values from -6 to 6
- patch_mask: int32 [512], replicated, may hold values 0 or 1
- gate_weight: bfloat16 [8192, 28672], P('col', 'row'), may hold values from -0.0625 to 0.0625
- up_weight: bfloat16 [8192, 28672], P('col', 'row'), may hold values from -0.0625 to 0.0625
- down_weight: bfloat16 [28672, 8192], P('row', 'col'), may hold values from -0.03125 to 0.03125
Outputs:
- clean_out: float32 [512, 8192], P('row', 'col')
- patched_out: float32 [512, 8192], P('row', 'col')
All inputs are finite; a program needn't handle non-finite values.
Results may differ from a plain program's by a relative error of at most 0.0029.
Values may be sent and summed in bfloat16 or wider, within the bound.
A program may use at most 128 MiB of HBM per device.

v0:
```python
import jax
import jax.numpy as jnp
from jax import lax
from jax.sharding import PartitionSpec as P


def on_device(clean_in, corrupt_in, patch_mask, gate_weight, up_weight, down_weight):
    stacked = jnp.stack((clean_in, corrupt_in), axis=1)
    piece = lax.all_gather(stacked, "row", axis=0, tiled=True)
    gate_part = jnp.einsum("tkd,df->tkf", piece, gate_weight, preferred_element_type=jnp.float32)
    up_part = jnp.einsum("tkd,df->tkf", piece, up_weight, preferred_element_type=jnp.float32)
    partial_sums = jnp.stack((gate_part, up_part), axis=2)
    summed = lax.psum_scatter(partial_sums, "col", scatter_dimension=0, tiled=True)
    row_count = summed.shape[0]
    row_mask = lax.dynamic_slice_in_dim(patch_mask, lax.axis_index("col") * row_count, row_count, 0)
    hidden = (jax.nn.silu(summed[:, :, 0]) * summed[:, :, 1]).astype(jnp.bfloat16)
    patched = jnp.where(row_mask[:, None] == 1, hidden[:, 0], hidden[:, 1])
    paired = jnp.stack((hidden[:, 0], patched), axis=1)
    gathered = lax.all_gather(paired, "col", axis=0, tiled=True)
    result = lax.psum_scatter(
        jnp.einsum("tkf,fd->tkd", gathered, down_weight, preferred_element_type=jnp.float32),
        "row",
        scatter_dimension=0,
        tiled=True,
    )
    return (result[:, 0], result[:, 1])


def solution(mesh):
    placed = (
        P("row", "col"),
        P("row", "col"),
        P(),
        P("col", "row"),
        P("col", "row"),
        P("row", "col"),
    )
    return jax.shard_map(
        on_device,
        mesh=mesh,
        in_specs=placed,
        out_specs=(P("row", "col"), P("row", "col")),
        check_vma=False,
    )
```

profile of v0, /device:TPU:2, one launch (start us, length us, event | category | flops | bytes accessed | tf_op | source)
XLA Modules:
  0.0 311.0 jit_solution(6040133685950640488)
XLA Ops:
  7.2 0.0 copy-start
  7.2 0.0 all-gather.3.cloned.1.call-start
  7.2 1.5 pad_maximum_fusion.2
  8.8 0.0 all-gather.3.cloned.1.call-update
  8.8 0.0 reduce-scatter.3.cloned.1.call-start
  8.8 43.1 %all-gather.3.cloned.1.call-done = bf16[512,2,512]{2,0,1:T(8,128)(2,1)} async-done(((bf16[32,2,512]{2,0,1:T(8,128)(2,1)}), bf16[512,2,512]{2,0,1:T(8,128)(2,1)}) %all-gather.3.cloned.1.call-update) | async-done | bytes 1048592 | tf_op jit(solution)/shard_map/all_gather | solution.py:9
  52.0 0.0 copy-done
  52.0 0.0 copy-start.1
  52.0 0.0 copy-start.2
  52.0 6.4 %convolution_bitcast_fusion = f32[512,2,1,1792]{3,0,1,2:T(8,128)} fusion(bf16[512,2,512]{2,0,1:T(8,128)(2,1)} %all-gather.3.cloned.1.call-done, bf16[512,1792]{1,0:T(8,128)(2,1)S(1)} %copy-done), kind=kOutput, calls=%fused_computation.1 | convolution fusion | flops 1879048192 | bytes 10223616 | tf_op jit(solution)/shard_map/tkd,df->tkf/dot_general | solution.py:11
  58.3 0.0 copy-done.1
  58.3 0.0 copy-done.2
  58.3 5.0 %convolution_bitcast_fusion.1 = f32[512,2,1,1792]{3,0,1,2:T(8,128)} fusion(bf16[512,2,512]{2,0,1:T(8,128)(2,1)S(1)} %copy-done.2, bf16[512,1792]{1,0:T(8,128)(2,1)S(1)} %copy-done.1), kind=kOutput, calls=%fused_computation.2 | convolution fusion | flops 1879048192 | bytes 10223616 | tf_op jit(solution)/shard_map/tkd,df->tkf/dot_general | solution.py:10
  63.4 11.9 %pad_maximum_fusion = f32[512,2,2,1792]{3,0,1,2:T(8,128)} fusion(f32[512,2,1,1792]{3,0,1,2:T(8,128)} %convolution_bitcast_fusion, f32[512,2,1,1792]{3,0,1,2:T(8,128)} %convolution_bitcast_fusion.1), kind=kLoop, calls=%fused_computation | loop fusion | flops 3670016 | bytes 29360128 | tf_op jit(solution)/shard_map/stack | solution.py:12
  75.3 0.0 reduce-scatter.3.cloned.1.call-update
  75.3 0.0 all-gather.5.cloned.1.call-start
  75.3 0.8 dynamic-slice_compare_fusion
  76.1 104.8 %reduce-scatter.3.cloned.1.call-done = f32[32,2,2,1792]{3,0,1,2:T(8,128)} async-done(((f32[512,2,2,1792]{3,0,1,2:T(8,128)}), f32[32,2,2,1792]{3,0,1,2:T(8,128)}) %reduce-scatter.3.cloned.1.call-update) | async-done | bytes 917520 | tf_op jit(solution)/shard_map/reduce_scatter | solution.py:13
  180.9 1.3 fusion.5
  182.2 0.1 fusion.6
  182.3 0.7 pad_maximum_fusion.1
  183.0 0.0 all-gather.5.cloned.1.call-update
  183.0 0.0 reduce-scatter.5.cloned.1.call-start
  183.1 54.0 %all-gather.5.cloned.1.call-done = bf16[512,2,1792]{2,0,1:T(8,128)(2,1)} async-done(((bf16[32,2,1792]{2,0,1:T(8,128)(2,1)}), bf16[512,2,1792]{2,0,1:T(8,128)(2,1)}) %all-gather.5.cloned.1.call-update) | async-done | bytes 3670032 | tf_op jit(solution)/shard_map/all_gather | solution.py:19
  237.0 6.0 %fusion = f32[512,2,512]{2,0,1:T(8,128)} fusion(bf16[512,2,1792]{2,0,1:T(8,128)(2,1)} %all-gather.5.cloned.1.call-done, bf16[1792,512]{1,0:T(8,128)(2,1)} %param.11), kind=kOutput, calls=%fused_computation.3 | convolution fusion | flops 1879048192 | bytes 7602176 | tf_op jit(solution)/shard_map/tkf,fd->tkd/dot_general | solution.py:21
  243.0 0.0 reduce-scatter.5.cloned.1.call-update
  243.1 59.8 %reduce-scatter.5.cloned.1.call-done = f32[32,2,512]{2,0,1:T(8,128)} async-done(((f32[512,2,512]{2,0,1:T(8,128)}), f32[32,2,512]{2,0,1:T(8,128)}) %reduce-scatter.5.cloned.1.call-update) | async-done | bytes 131088 | tf_op jit(solution)/shard_map/reduce_scatter | solution.py:20
  302.9 1.5 slice_bitcast_fusion.2
Async XLA Ops:
  7.2 44.8 %copy-start = (bf16[512,1792]{1,0:T(8,128)(2,1)S(1)}, bf16[512,1792]{1,0:T(8,128)(2,1)}, u32[]{:S(2)}) copy-start(bf16[512,1792]{1,0:T(8,128)(2,1)} %param.10) | copy-start | bytes 5505028
  7.2 44.8 %all-gather.3.cloned.1.call-start = ((), (), s32[]{:S(2)}) async-start(), calls=%async_computation.2 | async-start | bytes 1114112 | tf_op jit(solution)/shard_map/all_gather | solution.py:9
  8.8 172.1 %reduce-scatter.3.cloned.1.call-start = ((), (), s32[]{:S(2)}) async-start(), calls=%async_computation.3 | async-start | bytes 15597568 | tf_op jit(solution)/shard_map/reduce_scatter | solution.py:13
  52.0 6.4 %copy-start.1 = (bf16[512,1792]{1,0:T(8,128)(2,1)S(1)}, bf16[512,1792]{1,0:T(8,128)(2,1)}, u32[]{:S(2)}) copy-start(bf16[512,1792]{1,0:T(8,128)(2,1)} %param.9) | copy-start | bytes 5505028
  52.0 6.4 %copy-start.2 = (bf16[512,2,512]{2,0,1:T(8,128)(2,1)S(1)}, bf16[512,2,512]{2,0,1:T(8,128)(2,1)}, u32[]{:S(2)}) copy-start(bf16[512,2,512]{2,0,1:T(8,128)(2,1)} %all-gather.3.cloned.1.call-done) | copy-start | bytes 3145732
  75.3 161.8 %all-gather.5.cloned.1.call-start = ((), (), s32[]{:S(2)}) async-start(), calls=%async_computation.4 | async-start | bytes 3899392 | tf_op jit(solution)/shard_map/all_gather | solution.py:19
  183.0 119.9 %reduce-scatter.5.cloned.1.call-start = ((), (), s32[]{:S(2)}) async-start(), calls=%async_computation.5 | async-start | bytes 2228224 | tf_op jit(solution)/shard_map/reduce_scatter | solution.py:20
Sparse Core Ops, SparseCore 0:
  10.4 41.5 all-gather.2
  75.4 105.4 reduce-scatter.2
  183.3 53.6 all-gather.4
  243.2 59.6 reduce-scatter.4
where the time goes:
time: 311 us
  waiting for transfers between devices  262 us (84%)
  matrix products  17.4 us (6%)
  other arithmetic  16.3 us (5%)
  between operations  13.8 us (4%)
    reduce_scatter x1, waiting for transfers between devices, on_device(): lax.psum_scatter(partial_sums, 'col', scatter_dimension=0, tiled=True)  105 us
    reduce_scatter x1, waiting for transfers between devices, on_device(): lax.psum_scatter(jnp.einsum('tkf,fd->tkd', gathered, down_weight, preferr...  59.8 us
    all_gather x1, waiting for transfers between devices, on_device(): gathered = lax.all_gather(paired, 'col', axis=0, tiled=True)  54 us
    all_gather x1, waiting for transfers between devices, on_device(): piece = lax.all_gather(stacked, 'row', axis=0, tiled=True)  43.1 us
    another operation x1, other arithmetic, on_device(): partial_sums = jnp.stack((gate_part, up_part), axis=2)  11.9 us
    dot_general x1, matrix products, on_device(): jnp.einsum('tkd,df->tkf', piece, up_weight, preferred_element_type=jnp.fl...  6.36 us
  transfers between devices with their start and end apart: 4, of which 4 were waited for; matrix products, arithmetic and copies ran while one was open for 0% of the time, Pallas kernels for 0%

commit v1 on v0

--- a/solution.py
+++ b/solution.py
@@ -6,7 +6,9 @@
 
 def on_device(clean_in, corrupt_in, patch_mask, gate_weight, up_weight, down_weight):
     stacked = jnp.stack((clean_in, corrupt_in), axis=1)
-    piece = lax.all_gather(stacked, "row", axis=0, tiled=True)
+    piece = jnp.concatenate(
+        lax.all_to_all(jnp.stack([stacked] * lax.axis_size("row")), "row", 0, 0), axis=0
+    )
     gate_part = jnp.einsum("tkd,df->tkf", piece, gate_weight, preferred_element_type=jnp.float32)
     up_part = jnp.einsum("tkd,df->tkf", piece, up_weight, preferred_element_type=jnp.float32)
     partial_sums = jnp.stack((gate_part, up_part), axis=2)

time: 311 us -> 302 us (0.971)
  waiting for transfers between devices: 262 us -> 219 us
  blocking collectives: 0 us -> 35.5 us
    all_gather x1 -> x0, waiting for transfers between devices: 43.1 us -> none  [on_device(): piece = lax.all_gather(stacked, 'row', axis=0, tiled=True)]
    all_to_all x0 -> x1, blocking collectives: none -> 35.5 us  [on_device(): lax.all_to_all(jnp.stack([stacked] * lax.axis_size('row')), 'row', 0, 0)]
  transfers between devices with their start and end apart: 4 -> 3, of which waited for: 4 -> 3; matrix products, arithmetic and copies ran while one was open for 0% -> 0% of each run, Pallas kernels for 0% -> 0%
where the time goes in v1:
time: 302 us; the launch traced here: 301 us
  waiting for transfers between devices  219 us (73%)
  blocking collectives  35.5 us (12%)
  matrix products  16 us (5%)
  other arithmetic  15.6 us (5%)
  between operations  13.8 us (5%)
    reduce_scatter x1, waiting for transfers between devices, on_device(): lax.psum_scatter(partial_sums, 'col', scatter_dimension=0, tiled=True)  105 us
    reduce_scatter x1, waiting for transfers between devices, on_device(): lax.psum_scatter(jnp.einsum('tkf,fd->tkd', gathered, down_weight, preferr...  59.8 us
    all_gather x1, waiting for transfers between devices, on_device(): gathered = lax.all_gather(paired, 'col', axis=0, tiled=True)  54.1 us
    all_to_all x1, blocking collectives, on_device(): lax.all_to_all(jnp.stack([stacked] * lax.axis_size('row')), 'row', 0, 0)  35.5 us
    another operation x1, other arithmetic, on_device(): partial_sums = jnp.stack((gate_part, up_part), axis=2)  11.9 us
  transfers between devices with their start and end apart: 3, of which 3 were waited for; matrix products, arithmetic and copies ran while one was open for 0% of the time, Pallas kernels for 0%

profile of v1, /device:TPU:2, one launch (start us, length us, event | category | flops | bytes accessed | tf_op | source)
XLA Modules:
  0.0 301.4 jit_solution(8329041511735244777)
XLA Ops:
  7.2 0.0 copy-start
  7.2 0.0 reduce-scatter.3.cloned.1.call-start
  7.2 0.9 pad_maximum_fusion.2
  8.1 0.1 stack.19
  8.2 35.5 %all_to_all.5 = bf16[16,32,2,512]{3,1,2,0:T(8,128)(2,1)S(1)} all-to-all(bf16[16,32,2,512]{3,1,2,0:T(8,128)(2,1)S(1)} %stack.19), channel_id=1, replica_groups=mesh['row'=16,'col'=16] {'row'}, dimensions={0} | all-to-all | bytes 2097152 | tf_op jit(solution)/shard_map/all_to_all | solution.py:10
  43.8 0.1 copy.8
  43.9 0.0 copy-done
  43.9 0.0 copy-start.1
  43.9 5.0 %convolution_bitcast_fusion = f32[512,2,1,1792]{3,0,1,2:T(8,128)} fusion(bf16[512,2,512]{2,0,1:T(8,128)(2,1)S(1)} %bitcast.33, bf16[512,1792]{1,0:T(8,128)(2,1)S(1)} %copy-done), kind=kOutput, calls=%fused_computation.1 | convolution fusion | flops 1879048192 | bytes 10223616 | tf_op jit(solution)/shard_map/tkd,df->tkf/dot_general | solution.py:13
  48.9 0.0 copy-done.1
  48.9 5.0 %convolution_bitcast_fusion.1 = f32[512,2,1,1792]{3,0,1,2:T(8,128)} fusion(bf16[512,2,512]{2,0,1:T(8,128)(2,1)S(1)} %bitcast.34, bf16[512,1792]{1,0:T(8,128)(2,1)S(1)} %copy-done.1), kind=kOutput, calls=%fused_computation.2 | convolution fusion | flops 1879048192 | bytes 10223616 | tf_op jit(solution)/shard_map/tkd,df->tkf/dot_general | solution.py:12
  53.9 11.9 %pad_maximum_fusion = f32[512,2,2,1792]{3,0,1,2:T(8,128)} fusion(f32[512,2,1,1792]{3,0,1,2:T(8,128)} %convolution_bitcast_fusion, f32[512,2,1,1792]{3,0,1,2:T(8,128)} %convolution_bitcast_fusion.1), kind=kLoop, calls=%fused_computation | loop fusion | flops 3670016 | bytes 29360128 | tf_op jit(solution)/shard_map/stack | solution.py:14
  65.8 0.0 reduce-scatter.3.cloned.1.call-update
  65.9 0.0 all-gather.2.cloned.1.call-start
  65.9 0.8 dynamic-slice_compare_fusion
  66.7 104.6 %reduce-scatter.3.cloned.1.call-done = f32[32,2,2,1792]{3,0,1,2:T(8,128)} async-done(((f32[512,2,2,1792]{3,0,1,2:T(8,128)}), f32[32,2,2,1792]{3,0,1,2:T(8,128)}) %reduce-scatter.3.cloned.1.call-update) | async-done | bytes 917520 | tf_op jit(solution)/shard_map/reduce_scatter | solution.py:15
  171.3 1.3 fusion.5
  172.6 0.1 fusion.6
  172.7 0.7 pad_maximum_fusion.1
  173.4 0.0 all-gather.2.cloned.1.call-update
  173.4 0.0 reduce-scatter.5.cloned.1.call-start
  173.5 54.1 %all-gather.2.cloned.1.call-done = bf16[512,2,1792]{2,0,1:T(8,128)(2,1)} async-done(((bf16[32,2,1792]{2,0,1:T(8,128)(2,1)}), bf16[512,2,1792]{2,0,1:T(8,128)(2,1)}) %all-gather.2.cloned.1.call-update) | async-done | bytes 3670032 | tf_op jit(solution)/shard_map/all_gather | solution.py:21
  227.5 6.0 %fusion = f32[512,2,512]{2,0,1:T(8,128)} fusion(bf16[512,2,1792]{2,0,1:T(8,128)(2,1)} %all-gather.2.cloned.1.call-done, bf16[1792,512]{1,0:T(8,128)(2,1)} %param.11), kind=kOutput, calls=%fused_computation.3 | convolution fusion | flops 1879048192 | bytes 7602176 | tf_op jit(solution)/shard_map/tkf,fd->tkd/dot_general | solution.py:23
  233.5 0.0 reduce-scatter.5.cloned.1.call-update
  233.5 59.8 %reduce-scatter.5.cloned.1.call-done = f32[32,2,512]{2,0,1:T(8,128)} async-done(((f32[512,2,512]{2,0,1:T(8,128)}), f32[32,2,512]{2,0,1:T(8,128)}) %reduce-scatter.5.cloned.1.call-update) | async-done | bytes 131088 | tf_op jit(solution)/shard_map/reduce_scatter | solution.py:22
  293.4 1.5 slice_bitcast_fusion.2
Async XLA Ops:
  7.2 36.7 %copy-start = (bf16[512,1792]{1,0:T(8,128)(2,1)S(1)}, bf16[512,1792]{1,0:T(8,128)(2,1)}, u32[]{:S(2)}) copy-start(bf16[512,1792]{1,0:T(8,128)(2,1)} %param.10) | copy-start | bytes 5505028
  7.2 164.1 %reduce-scatter.3.cloned.1.call-start = ((), (), s32[]{:S(2)}) async-start(), calls=%async_computation.3 | async-start | bytes 15597568 | tf_op jit(solution)/shard_map/reduce_scatter | solution.py:15
  43.9 5.0 %copy-start.1 = (bf16[512,1792]{1,0:T(8,128)(2,1)S(1)}, bf16[512,1792]{1,0:T(8,128)(2,1)}, u32[]{:S(2)}) copy-start(bf16[512,1792]{1,0:T(8,128)(2,1)} %param.9) | copy-start | bytes 5505028
  65.9 161.7 %all-gather.2.cloned.1.call-start = ((), (), s32[]{:S(2)}) async-start(), calls=%async_computation.4 | async-start | bytes 3899392 | tf_op jit(solution)/shard_map/all_gather | solution.py:21
  173.4 120.0 %reduce-scatter.5.cloned.1.call-start = ((), (), s32[]{:S(2)}) async-start(), calls=%async_computation.5 | async-start | bytes 2228224 | tf_op jit(solution)/shard_map/reduce_scatter | solution.py:22
Sparse Core Ops, SparseCore 0:
  66.0 105.2 reduce-scatter.2
  173.8 53.7 all-gather.1
  233.7 59.6 reduce-scatter.4
